TPU v7x, 256 devices: a whole 4x4x8 slice. The times are simulated.
256 devices in a mesh: req: 64 (over x, z, core), tp: 4 (over y).
Axes of the slice: x: 4, y: 4, z: 8, core: 2. Of those that a mesh axis runs over, the one named last changes fastest.
Arguments:
- queries: bfloat16 [512, 2560], P('req', 'tp'), may hold values from -68 to 68, as said below
- new_kv: bfloat16 [512, 4, 256], P('req', 'tp'), may hold values from -6 to 6
- residual: bfloat16 [512, 2560], P('req', 'tp'), may hold values from -6 to 6
- kv_cache: bfloat16 [512, 512, 4, 256], P('req', None, 'tp'), may hold values from -6 to 6
- cache_len: int32 [512], P('req'), may hold values from 1 to 511, as said below
- request_perm: int32 [512], replicated, may hold values from 0 to 511, each once
- expert_ids: int32 [512, 6], P('req'), may hold values from 0 to 63, all different within a row; in each aligned block of 8 rows (0 to 7, 8 to 15, ...) at most 2 rows name the same one
- route_wt: float32 [512, 6], P('req'), may hold values from 0.05 to 1
- attn_out_w: bfloat16 [2560, 2560], P('tp'), may hold values from -0.125 to 0.125
- post_gain: float32 [2560], replicated, may hold values from 0.25 to 1.75
- expert_gate_up: bfloat16 [64, 2, 2560, 1536], P('req', None, None, 'tp'), may hold values from -0.125 to 0.125
- expert_down: bfloat16 [64, 1536, 2560], P('req', 'tp'), may hold values from -0.15625 to 0.15625
- final_gain: float32 [2560], replicated, may hold values from 0.25 to 1.75
- vocab_w: bfloat16 [103424, 2560], P(('req', 'tp')), may hold values from -0.125 to 0.125
Outputs:
- hidden_out: bfloat16 [512, 2560], P('req', 'tp')
- state_norm: float32 [512], P('req')
- top_logit: float32 [512], P('req')
Inputs may be any that keep to these rules, and one draw needn't show every extreme that they name: queries lie within this range. Slot s holds cache_len[s] filled rows; some slot holds exactly 511. `request_perm`: a permutation of the slots. `expert_ids`: each row names 6 different experts; among the rows of one device (aligned blocks of 8 rows) no expert is named more than 2 times, and in some block one expert is named exactly 2 times.
All inputs are finite; a program needn't handle non-finite values.
Results may differ from a plain program's by a relative error of at most 0.007.
Values may be sent and summed in bfloat16 or wider, within the bound.
No kernel may reach another device: no remote copies, remote signals or barrier semaphores. Data moves between devices by JAX's collectives and lax.ppermute only.
A program may use at most 64 MiB of HBM per device.

v0:
```python
import jax
import jax.numpy as jnp
from jax import lax
from jax.sharding import PartitionSpec as P

epsilon = 1e-05


def attend(queries, fresh_kv, kv_block, lengths, head_dim):
    slot_count, context, kv_heads, _ = kv_block.shape
    groups = queries.shape[1] // head_dim // kv_heads
    query_heads = queries.reshape(slot_count, kv_heads, groups, head_dim)
    key_part = kv_block[..., :head_dim]
    value_part = kv_block[..., head_dim:]
    score_scale = head_dim ** (-0.5)
    scores = (
        jnp.einsum("skgd,sckd->skgc", query_heads, key_part, preferred_element_type=jnp.float32)
        * score_scale
    )
    live_mask = (jnp.arange(context, dtype=jnp.int32)[None, :] < lengths[:, None])[:, None, None, :]
    scores = jnp.where(live_mask, scores, -1e30)
    own_score = (
        jnp.einsum(
            "skgd,skd->skg",
            query_heads,
            fresh_kv[..., :head_dim],
            preferred_element_type=jnp.float32,
        )
        * score_scale
    )
    highest = jnp.maximum(jnp.max(scores, axis=-1), own_score)
    weights = jnp.where(live_mask, jnp.exp(scores - highest[..., None]), 0.0)
    own_weight = jnp.exp(own_score - highest)
    total_weight = jnp.sum(weights, axis=-1) + own_weight
    own_round = lax.optimization_barrier(own_weight.astype(jnp.bfloat16)).astype(jnp.float32)
    mixed_sum = jnp.einsum(
        "skgc,sckd->skgd",
        weights.astype(jnp.bfloat16),
        value_part,
        preferred_element_type=jnp.float32,
    )
    mixed_sum = mixed_sum + own_round[..., None] * fresh_kv[:, :, None, head_dim:].astype(
        jnp.float32
    )
    return (mixed_sum / total_weight[..., None]).reshape(slot_count, -1).astype(jnp.bfloat16)


def expert_rows(inputs, gate_up, down_proj):
    gate_val = jnp.dot(inputs, gate_up[0], preferred_element_type=jnp.float32)
    upward = jnp.dot(inputs, gate_up[1], preferred_element_type=jnp.float32)
    active = (jax.nn.silu(gate_val) * upward).astype(jnp.bfloat16)
    return jnp.dot(active, down_proj, preferred_element_type=jnp.float32)


def send_back(results):
    return lax.all_to_all(
        results.astype(jnp.bfloat16), "req", split_axis=0, concat_axis=0, tiled=True
    ).astype(results.dtype)


def on_device(
    queries,
    new_kv,
    residual,
    kv_cache,
    cache_len,
    request_perm,
    expert_ids,
    route_wt,
    attn_out_w,
    post_gain,
    expert_gate_up,
    expert_down,
    final_gain,
    vocab_w,
):
    group_count = lax.axis_size("req")
    group_index = lax.axis_index("req")
    member = lax.axis_index("tp")
    local_rows = queries.shape[0]
    top_count = expert_ids.shape[1]
    col_width = residual.shape[1]
    model_width = attn_out_w.shape[1]
    head_dim = new_kv.shape[2] // 2
    capacity = max(2, (local_rows * top_count + group_count - 1) // group_count)
    dealt_q, dealt_kv, dealt_res = (
        lax.all_gather(queries, "req", axis=0, tiled=True),
        lax.all_gather(new_kv, "req", axis=0, tiled=True),
        lax.all_gather(residual, "req", axis=0, tiled=True),
    )
    total_rows = dealt_q.shape[0]
    slot_ids = group_index * local_rows + jnp.arange(local_rows, dtype=jnp.int32)
    pick_rows = (request_perm[None, :] == slot_ids[:, None]).astype(jnp.bfloat16)
    mine_q = jnp.dot(pick_rows, dealt_q, preferred_element_type=jnp.float32).astype(jnp.bfloat16)
    mine_kv = jnp.dot(
        pick_rows, dealt_kv.reshape(total_rows, -1), preferred_element_type=jnp.float32
    )
    mine_kv = mine_kv.astype(jnp.bfloat16).reshape(new_kv.shape)
    mine_res = jnp.dot(pick_rows, dealt_res, preferred_element_type=jnp.float32)
    attended = attend(mine_q, mine_kv, kv_cache, cache_len, head_dim)
    partial_value = jnp.dot(attended, attn_out_w, preferred_element_type=jnp.float32)
    col_start = member * col_width
    own_part = lax.dynamic_slice_in_dim(partial_value, col_start, col_width, 1) + mine_res
    summand = lax.dynamic_update_slice_in_dim(partial_value, own_part, col_start, 1)
    mixed_full = lax.psum(summand, "tp")
    scale_rows = lax.rsqrt(jnp.mean(mixed_full * mixed_full, axis=1, keepdims=True) + epsilon)
    normed = (mixed_full * scale_rows * post_gain).astype(jnp.bfloat16)
    mixed_cols = lax.dynamic_slice_in_dim(mixed_full, col_start, col_width, 1)
    expert_axis = jnp.arange(group_count, dtype=jnp.int32)
    hit_table = (
        (expert_ids[..., None] == expert_axis)
        .astype(jnp.int32)
        .reshape(local_rows * top_count, group_count)
    )
    earlier = jnp.cumsum(hit_table, axis=0) - hit_table
    slot_rank = jnp.sum(earlier * hit_table, axis=1)
    target = expert_ids.reshape(-1) * capacity + slot_rank
    slot_axis = jnp.arange(group_count * capacity, dtype=jnp.int32)
    matches = (slot_axis[:, None] == target[None, :]).astype(jnp.float32)
    matches = matches.reshape(group_count * capacity, local_rows, top_count)
    route_share = route_wt / jnp.sum(route_wt, axis=1, keepdims=True)
    blending = jnp.sum(matches * route_share[None], axis=2).T
    gate_up = expert_gate_up[0]
    down_proj = expert_down[0]
    every_row = lax.all_gather(normed, "req", axis=0, tiled=True)
    every_id = lax.all_gather(expert_ids, "req", axis=0, tiled=True)
    all_hits = (every_id[..., None] == expert_axis).astype(jnp.int32)
    all_hits = all_hits.reshape(group_count, local_rows * top_count, group_count)
    all_prior = jnp.cumsum(all_hits, axis=1) - all_hits
    all_rank = jnp.sum(all_prior * all_hits, axis=2)
    own_routes = every_id.reshape(group_count, local_rows * top_count) == group_index
    cap_axis = jnp.arange(capacity, dtype=jnp.int32)
    chosen = (own_routes[..., None] & (all_rank[..., None] == cap_axis)).astype(jnp.float32)
    chosen = jnp.sum(chosen.reshape(group_count, local_rows, top_count, capacity), axis=2).astype(
        jnp.bfloat16
    )
    inbound = jnp.einsum(
        "btc,btd->bcd",
        chosen,
        every_row.reshape(group_count, local_rows, model_width),
        preferred_element_type=jnp.float32,
    )
    inbound = inbound.astype(jnp.bfloat16)
    produced = expert_rows(inbound.reshape(group_count * capacity, model_width), gate_up, down_proj)
    returned = send_back(produced.reshape(group_count, capacity, model_width))
    moe_part = jnp.dot(
        blending,
        returned.reshape(group_count * capacity, model_width),
        precision=lax.Precision.HIGHEST,
        preferred_element_type=jnp.float32,
    )
    moe_cols = lax.psum_scatter(
        moe_part.astype(jnp.bfloat16), "tp", scatter_dimension=1, tiled=True
    ).astype(jnp.float32)
    state_cols = (mixed_cols + moe_cols).astype(jnp.bfloat16)
    state_row = lax.all_gather(state_cols, "tp", axis=1, tiled=True)
    every_state = lax.all_gather(state_row, "req", axis=0, tiled=True)
    wanted = lax.dynamic_slice_in_dim(request_perm, group_index * local_rows, local_rows)
    back_pick = wanted[:, None] == jnp.arange(total_rows, dtype=jnp.int32)[None, :]
    own_rows = jnp.dot(
        back_pick.astype(jnp.bfloat16), every_state, preferred_element_type=jnp.float32
    )
    hidden_out = lax.dynamic_slice_in_dim(own_rows, col_start, col_width, 1).astype(jnp.bfloat16)
    state_norm = jnp.sqrt(jnp.mean(own_rows * own_rows, axis=1) + epsilon)
    every_flat = every_state.astype(jnp.float32)
    ready_rows = (
        every_flat
        * lax.rsqrt(jnp.mean(every_flat * every_flat, axis=1, keepdims=True) + epsilon)
        * final_gain
    ).astype(jnp.bfloat16)
    logits = lax.dot_general(
        ready_rows, vocab_w, (((1,), (1,)), ((), ())), preferred_element_type=jnp.float32
    )
    local_top = jnp.max(logits, axis=1)
    global_top = lax.pmax(local_top, ("req", "tp"))
    top_logit = jnp.sum(jnp.where(back_pick, global_top[None, :], 0.0), axis=1)
    return (hidden_out, state_norm, top_logit)


def solution(mesh):
    placed = (
        P("req", "tp"),
        P("req", "tp", None),
        P("req", "tp"),
        P("req", None, "tp", None),
        P("req"),
        P(),
        P("req", None),
        P("req", None),
        P("tp", None),
        P(),
        P("req", None, None, "tp"),
        P("req", "tp", None),
        P(),
        P(("req", "tp"), None),
    )
    return jax.shard_map(
        on_device,
        mesh=mesh,
        in_specs=placed,
        out_specs=(P("req", "tp"), P("req"), P("req")),
        check_vma=False,
    )
```

profile of v0, /device:TPU:1, one launch (start us, length us, event | category | flops | bytes accessed | tf_op | source)
XLA Modules:
  0.0 543.5 jit_solution(1999221724259459225)
XLA Ops:
  7.3 55.1 %all_gather.21 = bf16[512,640]{1,0:T(8,128)(2,1)S(1)} all-gather(bf16[8,640]{1,0:T(8,128)(2,1)} %param.14), channel_id=1, replica_groups=mesh['req'=64,'tp'=4] {'req'}, dimensions={0}, use_global_device_ids=true | all-gather | bytes 665600 | tf_op jit(solution)/shard_map/all_gather | solution.py:87
  62.4 43.1 %all_gather.22 = bf16[512,1,256]{2,0,1:T(8,128)(2,1)S(1)} all-gather(bf16[8,1,256]{2,0,1:T(8,128)(2,1)} %param.15), channel_id=1, replica_groups=mesh['req'=64,'tp'=4] {'req'}, dimensions={0}, use_global_device_ids=true | all-gather | bytes 266240 | tf_op jit(solution)/shard_map/all_gather | solution.py:88
  108.1 1.7 fusion.69
  110.0 52.5 %all_gather.23 = bf16[512,640]{1,0:T(8,128)(2,1)} all-gather(bf16[8,640]{1,0:T(8,128)(2,1)S(1)} %copy-done.7), channel_id=1, replica_groups=mesh['req'=64,'tp'=4] {'req'}, dimensions={0}, use_global_device_ids=true | all-gather | bytes 665600 | tf_op jit(solution)/shard_map/all_gather | solution.py:89
  162.5 1.5 fusion.33
  164.7 1.3 fusion.32
  166.7 40.7 %all-reduce.2.cloned.1.call-done = f32[8,2560]{1,0:T(8,128)} async-done(((f32[8,2560]{1,0:T(8,128)}), f32[8,2560]{1,0:T(8,128)}) %all-reduce.2.cloned.1.call-update) | async-done | bytes 81936 | tf_op jit(solution)/shard_map/psum | solution.py:105
  207.4 1.0 multiply_reduce_fusion.1
  208.5 1.6 multiply_convert_fusion
  210.1 47.8 %all_gather.24 = s32[512,6]{1,0:T(8,128)S(1)} all-gather(s32[8,6]{1,0:T(8,128)S(1)} %copy-done.4), channel_id=1, replica_groups=mesh['req'=64,'tp'=4] {'req'}, dimensions={0}, use_global_device_ids=true | all-gather | bytes 12480 | tf_op jit(solution)/shard_map/all_gather | solution.py:126
  259.2 1.0 copy.41
  261.1 1.7 fusion.68
  262.9 28.5 %all-gather.3.cloned.1.call-done = bf16[512,2560]{1,0:T(8,128)(2,1)} async-done(((bf16[8,2560]{1,0:T(8,128)(2,1)}), bf16[512,2560]{1,0:T(8,128)(2,1)}) %all-gather.3.cloned.1.call-update) | async-done | bytes 2621456 | tf_op jit(solution)/shard_map/all_gather | solution.py:125
  291.4 3.4 convolution_convert_fusion
  294.8 2.7 reshape.188
  297.6 2.3 fusion.13
  299.9 2.1 fusion.26
  302.0 2.1 convolution_convert_fusion.1
  304.1 1.5 copy.46
  305.6 6.7 %all-to-all-start = ((bf16[64,2,2560]{2,1,0:T(2,128)(2,1)}), bf16[64,2,2560]{2,1,0:T(2,128)(2,1)}, u32[]{:S(2)}, u32[]{:S(2)}) async-start(bf16[64,2,2560]{2,1,0:T(2,128)(2,1)} %copy.46), calls=%async_computation | async-start | bytes 1310720 | tf_op jit(solution)/shard_map/all_to_all | solution.py:56
  313.3 19.0 %all-to-all-done = bf16[64,2,2560]{2,1,0:T(2,128)(2,1)} async-done(((bf16[64,2,2560]{2,1,0:T(2,128)(2,1)}), bf16[64,2,2560]{2,1,0:T(2,128)(2,1)}, u32[]{:S(2)}, u32[]{:S(2)}) %all-to-all-start) | async-done | bytes 655392 | tf_op jit(solution)/shard_map/all_to_all | solution.py:56
  332.4 2.7 reshape.189
  335.1 1.4 convolution_convert_fusion.2
  336.5 1.1 copy.49
  337.7 20.3 %reduce-scatter.4.cloned.1.call-done = bf16[640,8]{1,0:T(8,128)(2,1)} async-done(((bf16[2560,8]{1,0:T(8,128)(2,1)}), bf16[640,8]{1,0:T(8,128)(2,1)}) %reduce-scatter.4.cloned.1.call-update) | async-done | bytes 10256
  358.0 1.0 copy.50
  359.7 9.9 %all_gather.26 = bf16[8,2560]{1,0:T(8,128)(2,1)} all-gather(bf16[8,640]{1,0:T(8,128)(2,1)S(1)} %add_convert_fusion), channel_id=1, replica_groups=mesh['req'=64,'tp'=4] {'tp'}, dimensions={1}, use_global_device_ids=true | all-gather | bytes 51200 | tf_op jit(solution)/shard_map/all_gather | solution.py:156
  369.8 82.1 %all-gather.5.cloned.1.call-done = bf16[512,2560]{1,0:T(8,128)(2,1)} async-done(((bf16[8,2560]{1,0:T(8,128)(2,1)}), bf16[512,2560]{1,0:T(8,128)(2,1)}) %all-gather.5.cloned.1.call-update) | async-done | bytes 2621456 | tf_op jit(solution)/shard_map/all_gather | solution.py:157
  451.9 2.5 fusion
  454.4 3.0 fusion.20
  457.4 75.4 %pmax.7 = f32[512]{0:T(512)S(1)} all-reduce(f32[512]{0:T(512)S(1)} %fusion.20), channel_id=1, replica_groups=mesh['req'=64,'tp'=4] {'req','tp'}, use_global_device_ids=true, to_apply=%region_15.16 | all-reduce | flops 512 | bytes 4096 | tf_op jit(solution)/shard_map/pmax | solution.py:175
  533.5 2.3 multiply_reduce_fusion
  (65 shorter events, 10.4 us)
Async XLA Ops:
  7.2 156.9 %copy-start = (bf16[640,2560]{1,0:T(8,128)(2,1)S(1)}, bf16[640,2560]{1,0:T(8,128)(2,1)}, u32[]{:S(2)}) copy-start(bf16[640,2560]{1,0:T(8,128)(2,1)} %param.22) | copy-start | bytes 9830404
  7.2 102.8 %copy-start.7 = (bf16[8,640]{1,0:T(8,128)(2,1)S(1)}, bf16[8,640]{1,0:T(8,128)(2,1)}, u32[]{:S(2)}) copy-start(bf16[8,640]{1,0:T(8,128)(2,1)} %param.16) | copy-start | bytes 30724
  7.2 200.2 %all-reduce.2.cloned.1.call-start = ((), (), s32[]{:S(2)}) async-start(), calls=%async_computation.2 | async-start | bytes 163840 | tf_op jit(solution)/shard_map/psum | solution.py:105
  162.5 2.1 copy-start.8
  164.1 44.4 %copy-start.6 = (f32[2560]{0:T(1024)S(1)}, f32[2560]{0:T(1024)}, u32[]{:S(2)}) copy-start(f32[2560]{0:T(1024)} %param.23) | copy-start | bytes 30724
  164.1 46.0 %copy-start.4 = (s32[8,6]{1,0:T(8,128)S(1)}, s32[8,6]{1,0:T(8,128)}, u32[]{:S(2)}) copy-start(s32[8,6]{1,0:T(8,128)} %param.20) | copy-start | bytes 580
  166.0 0.6 copy-start.3
  166.6 124.8 %all-gather.3.cloned.1.call-start = ((), (), s32[]{:S(2)}) async-start(), calls=%async_computation.3 | async-start | bytes 2662400 | tf_op jit(solution)/shard_map/all_gather | solution.py:125
  297.5 2.3 copy-start.2
  302.0 10.9 %copy-start.5 = (f32[8,6]{1,0:T(8,128)S(1)}, f32[8,6]{1,0:T(8,128)}, u32[]{:S(2)}) copy-start(f32[8,6]{1,0:T(8,128)} %param.21) | copy-start | bytes 580
  305.6 26.7 %all-to-all-start = ((bf16[64,2,2560]{2,1,0:T(2,128)(2,1)}), bf16[64,2,2560]{2,1,0:T(2,128)(2,1)}, u32[]{:S(2)}, u32[]{:S(2)}) async-start(bf16[64,2,2560]{2,1,0:T(2,128)(2,1)} %copy.46), calls=%async_computation | async-start | bytes 1310720 | tf_op jit(solution)/shard_map/all_to_all | solution.py:56
  312.3 45.7 %reduce-scatter.4.cloned.1.call-start = ((), (), s32[]{:S(2)}) async-start(), calls=%async_computation.5 | async-start | bytes 819200
  336.5 117.8 %copy-start.9 = (f32[2560]{0:T(1024)S(1)}, f32[2560]{0:T(1024)}, u32[]{:S(2)}) copy-start(f32[2560]{0:T(1024)} %param.26) | copy-start | bytes 30724
  337.6 114.2 %all-gather.5.cloned.1.call-start = ((), (), s32[]{:S(2)}) async-start(), calls=%async_computation.4 | async-start | bytes 2662400 | tf_op jit(solution)/shard_map/all_gather | solution.py:157
  451.9 2.5 copy-start.1
Sparse Core Ops, SparseCore 0:
  166.8 40.6 all-reduce.1
  210.6 80.8 all-gather.2
  337.8 20.1 reduce-scatter.3
  369.8 82.0 all-gather.4
where the time goes:
time: 545 us; the launch traced here: 544 us
  blocking collectives  284 us (52%)
  waiting for transfers between devices  191 us (35%)
  matrix products  23.6 us (4%)
  between operations  14 us (3%)
  local copies, waits for them, and re-layouts  13.5 us (2%)
  other arithmetic  11 us (2%)
  starting transfers between devices  6.83 us (1%)
    all_gather x1, waiting for transfers between devices, on_device(): every_state = lax.all_gather(state_row, 'req', axis=0, tiled=True)  82.1 us
    pmax x1, blocking collectives, on_device(): global_top = lax.pmax(local_top, ('req', 'tp'))  75.4 us
    all_gather x1, blocking collectives, on_device(): lax.all_gather(queries, 'req', axis=0, tiled=True)  55.1 us
    all_gather x1, blocking collectives, on_device(): lax.all_gather(residual, 'req', axis=0, tiled=True)  52.5 us
    all_gather x1, blocking collectives, on_device(): every_id = lax.all_gather(expert_ids, 'req', axis=0, tiled=True)  47.8 us
    all_gather x1, blocking collectives, on_device(): lax.all_gather(new_kv, 'req', axis=0, tiled=True)  43.1 us
    psum x1, waiting for transfers between devices, on_device(): mixed_full = lax.psum(summand, 'tp')  40.7 us
    all_gather x1, waiting for transfers between devices, on_device(): every_row = lax.all_gather(normed, 'req', axis=0, tiled=True)  28.5 us
  transfers between devices with their start and end apart: 5, of which 5 were waited for; matrix products, arithmetic and copies ran while one was open for 1% of the time, Pallas kernels for 0%

commit v1 on v0

--- a/solution.py
+++ b/solution.py
@@ -85,7 +85,9 @@
     capacity = max(2, (local_rows * top_count + group_count - 1) // group_count)
     dealt_q, dealt_kv, dealt_res = (
         lax.all_gather(queries, "req", axis=0, tiled=True),
-        lax.all_gather(new_kv, "req", axis=0, tiled=True),
+        jnp.concatenate(
+            lax.all_to_all(jnp.stack([new_kv] * lax.axis_size("req")), "req", 0, 0), axis=0
+        ),
         lax.all_gather(residual, "req", axis=0, tiled=True),
     )
     total_rows = dealt_q.shape[0]

time: 545 us -> 513 us (0.941)
  blocking collectives: 284 us -> 239 us
  starting transfers between devices: 6.83 us -> 20 us
    all_gather x1 -> x0, blocking collectives: 43.1 us -> none  [on_device(): lax.all_gather(new_kv, 'req', axis=0, tiled=True)]
    all_to_all x0 -> x1, starting transfers between devices: none -> 13.2 us  [on_device(): lax.all_to_all(jnp.stack([new_kv] * lax.axis_size('req')), 'req', 0, 0)]
  transfers between devices with their start and end apart: 5 -> 6, of which waited for: 5 -> 5; matrix products, arithmetic and copies ran while one was open for 1% -> 2% of each run, Pallas kernels for 0% -> 0%
where the time goes in v1:
time: 513 us; the launch traced here: 512 us
  blocking collectives  239 us (47%)
  waiting for transfers between devices  191 us (37%)
  matrix products  22.2 us (4%)
  starting transfers between devices  20 us (4%)
  local copies, waits for them, and re-layouts  15 us (3%)
  between operations  14 us (3%)
  other arithmetic  10.4 us (2%)
    all_gather x1, waiting for transfers between devices, on_device(): every_state = lax.all_gather(state_row, 'req', axis=0, tiled=True)  82.3 us
    pmax x1, blocking collectives, on_device(): global_top = lax.pmax(local_top, ('req', 'tp'))  75.4 us
    all_gather x1, blocking collectives, on_device(): lax.all_gather(residual, 'req', axis=0, tiled=True)  53.9 us
    all_gather x1, blocking collectives, on_device(): lax.all_gather(queries, 'req', axis=0, tiled=True)  52.1 us
    all_gather x1, blocking collectives, on_device(): every_id = lax.all_gather(expert_ids, 'req', axis=0, tiled=True)  47.8 us
    psum x1, waiting for transfers between devices, on_device(): mixed_full = lax.psum(summand, 'tp')  41.7 us
    all_gather x1, waiting for transfers between devices, on_device(): every_row = lax.all_gather(normed, 'req', axis=0, tiled=True)  28.5 us
    unnamed x5, waiting for transfers between devices  19.8 us
  transfers between devices with their start and end apart: 6, of which 5 were waited for; matrix products, arithmetic and copies ran while one was open for 2% of the time, Pallas kernels for 0%

profile of v1, /device:TPU:1, one launch (start us, length us, event | category | flops | bytes accessed | tf_op | source)
XLA Modules:
  0.0 512.3 jit_solution(13020805028642715624)
XLA Ops:
  7.2 1.5 stack.2
  8.7 13.2 %all-to-all-start = ((bf16[64,8,1,256]{3,1,2,0:T(8,128)(2,1)}), bf16[64,8,1,256]{3,1,2,0:T(8,128)(2,1)}, u32[]{:S(2)}, u32[]{:S(2)}) async-start(bf16[64,8,1,256]{3,1,2,0:T(8,128)(2,1)} %stack.2), calls=%async_computation | async-start | bytes 524288 | tf_op jit(solution)/shard_map/all_to_all | solution.py:89
  22.0 52.1 %all_gather.18 = bf16[512,640]{1,0:T(8,128)(2,1)S(1)} all-gather(bf16[8,640]{1,0:T(8,128)(2,1)} %param.14), channel_id=1, replica_groups=mesh['req'=64,'tp'=4] {'req'}, dimensions={0}, use_global_device_ids=true | all-gather | bytes 665600 | tf_op jit(solution)/shard_map/all_gather | solution.py:87
  74.0 53.9 %all_gather.19 = bf16[512,640]{1,0:T(8,128)(2,1)} all-gather(bf16[8,640]{1,0:T(8,128)(2,1)} %param.16), channel_id=1, replica_groups=mesh['req'=64,'tp'=4] {'req'}, dimensions={0}, use_global_device_ids=true | all-gather | bytes 665600 | tf_op jit(solution)/shard_map/all_gather | solution.py:91
  128.3 1.7 fusion.69
  130.0 1.1 fusion.35
  131.5 1.6 fusion.33
  134.6 41.7 %all-reduce.2.cloned.1.call-done = f32[8,2560]{1,0:T(8,128)} async-done(((f32[8,2560]{1,0:T(8,128)}), f32[8,2560]{1,0:T(8,128)}) %all-reduce.2.cloned.1.call-update) | async-done | bytes 81936 | tf_op jit(solution)/shard_map/psum | solution.py:107
  176.3 1.0 multiply_reduce_fusion.1
  177.3 1.6 multiply_convert_fusion
  178.9 47.8 %all_gather.20 = s32[512,6]{1,0:T(8,128)S(1)} all-gather(s32[8,6]{1,0:T(8,128)S(1)} %copy-done.5), channel_id=1, replica_groups=mesh['req'=64,'tp'=4] {'req'}, dimensions={0}, use_global_device_ids=true | all-gather | bytes 12480 | tf_op jit(solution)/shard_map/all_gather | solution.py:128
  229.9 1.7 fusion.68
  231.8 28.5 %all-gather.3.cloned.1.call-done = bf16[512,2560]{1,0:T(8,128)(2,1)} async-done(((bf16[8,2560]{1,0:T(8,128)(2,1)}), bf16[512,2560]{1,0:T(8,128)(2,1)}) %all-gather.3.cloned.1.call-update) | async-done | bytes 2621456 | tf_op jit(solution)/shard_map/all_gather | solution.py:127
  260.3 3.4 convolution_convert_fusion
  263.7 2.7 reshape.187
  266.4 2.3 fusion.13
  268.7 2.1 fusion.26
  270.8 2.0 convolution_convert_fusion.1
  272.9 1.5 copy.46
  274.4 6.7 %all-to-all-start.1 = ((bf16[64,2,2560]{2,1,0:T(2,128)(2,1)}), bf16[64,2,2560]{2,1,0:T(2,128)(2,1)}, u32[]{:S(2)}, u32[]{:S(2)}) async-start(bf16[64,2,2560]{2,1,0:T(2,128)(2,1)} %copy.46), calls=%async_computation.1 | async-start | bytes 1310720 | tf_op jit(solution)/shard_map/all_to_all | solution.py:56
  282.1 19.0 %all-to-all-done.1 = bf16[64,2,2560]{2,1,0:T(2,128)(2,1)} async-done(((bf16[64,2,2560]{2,1,0:T(2,128)(2,1)}), bf16[64,2,2560]{2,1,0:T(2,128)(2,1)}, u32[]{:S(2)}, u32[]{:S(2)}) %all-to-all-start.1) | async-done | bytes 655392 | tf_op jit(solution)/shard_map/all_to_all | solution.py:56
  301.2 2.7 reshape.188
  303.9 1.4 convolution_convert_fusion.2
  305.3 1.1 copy.49
  306.5 19.8 %reduce-scatter.4.cloned.1.call-done = bf16[640,8]{1,0:T(8,128)(2,1)} async-done(((bf16[2560,8]{1,0:T(8,128)(2,1)}), bf16[640,8]{1,0:T(8,128)(2,1)}) %reduce-scatter.4.cloned.1.call-update) | async-done | bytes 10256
  326.3 1.0 copy.50
  328.0 10.3 %all_gather.22 = bf16[8,2560]{1,0:T(8,128)(2,1)} all-gather(bf16[8,640]{1,0:T(8,128)(2,1)S(1)} %add_convert_fusion), channel_id=1, replica_groups=mesh['req'=64,'tp'=4] {'tp'}, dimensions={1}, use_global_device_ids=true | all-gather | bytes 51200 | tf_op jit(solution)/shard_map/all_gather | solution.py:158
  338.4 82.3 %all-gather.5.cloned.1.call-done = bf16[512,2560]{1,0:T(8,128)(2,1)} async-done(((bf16[8,2560]{1,0:T(8,128)(2,1)}), bf16[512,2560]{1,0:T(8,128)(2,1)}) %all-gather.5.cloned.1.call-update) | async-done | bytes 2621456 | tf_op jit(solution)/shard_map/all_gather | solution.py:159
  420.6 2.5 fusion
  423.2 3.0 fusion.20
  426.2 75.4 %pmax.7 = f32[512]{0:T(512)S(1)} all-reduce(f32[512]{0:T(512)S(1)} %fusion.20), channel_id=1, replica_groups=mesh['req'=64,'tp'=4] {'req','tp'}, use_global_device_ids=true, to_apply=%region_15.16 | all-reduce | flops 512 | bytes 4096 | tf_op jit(solution)/shard_map/pmax | solution.py:177
  502.3 2.3 multiply_reduce_fusion
  (69 shorter events, 9.4 us)
Async XLA Ops:
  7.2 125.9 %copy-start = (bf16[640,2560]{1,0:T(8,128)(2,1)S(1)}, bf16[640,2560]{1,0:T(8,128)(2,1)}, u32[]{:S(2)}) copy-start(bf16[640,2560]{1,0:T(8,128)(2,1)} %param.22) | copy-start | bytes 9830404
  7.2 120.8 %copy-start.8 = (s32[512]{0:T(512)S(1)}, s32[512]{0:T(512)}, u32[]{:S(2)}) copy-start(s32[512]{0:T(512)} %param.19) | copy-start | bytes 6148
  7.2 121.0 %copy-start.9 = (s32[8]{0:T(128)S(1)}, s32[8]{0:T(128)}, u32[]{:S(2)}) copy-start(s32[8]{0:T(128)} %param.18) | copy-start | bytes 100
  8.7 121.2 %all-to-all-start = ((bf16[64,8,1,256]{3,1,2,0:T(8,128)(2,1)}), bf16[64,8,1,256]{3,1,2,0:T(8,128)(2,1)}, u32[]{:S(2)}, u32[]{:S(2)}) async-start(bf16[64,8,1,256]{3,1,2,0:T(8,128)(2,1)} %stack.2), calls=%async_computation | async-start | bytes 524288 | tf_op jit(solution)/shard_map/all_to_all | solution.py:89
  21.9 154.3 %all-reduce.2.cloned.1.call-start = ((), (), s32[]{:S(2)}) async-start(), calls=%async_computation.3 | async-start | bytes 163840 | tf_op jit(solution)/shard_map/psum | solution.py:107
  131.5 2.2 copy-start.2
  133.1 44.2 %copy-start.7 = (f32[2560]{0:T(1024)S(1)}, f32[2560]{0:T(1024)}, u32[]{:S(2)}) copy-start(f32[2560]{0:T(1024)} %param.23) | copy-start | bytes 30724
  133.1 45.8 %copy-start.5 = (s32[8,6]{1,0:T(8,128)S(1)}, s32[8,6]{1,0:T(8,128)}, u32[]{:S(2)}) copy-start(s32[8,6]{1,0:T(8,128)} %param.20) | copy-start | bytes 580
  133.9 0.6 copy-start.4
  134.6 125.7 %all-gather.3.cloned.1.call-start = ((), (), s32[]{:S(2)}) async-start(), calls=%async_computation.4 | async-start | bytes 2662400 | tf_op jit(solution)/shard_map/all_gather | solution.py:127
  266.4 2.3 copy-start.3
  270.8 10.9 %copy-start.6 = (f32[8,6]{1,0:T(8,128)S(1)}, f32[8,6]{1,0:T(8,128)}, u32[]{:S(2)}) copy-start(f32[8,6]{1,0:T(8,128)} %param.21) | copy-start | bytes 580
  274.4 26.8 %all-to-all-start.1 = ((bf16[64,2,2560]{2,1,0:T(2,128)(2,1)}), bf16[64,2,2560]{2,1,0:T(2,128)(2,1)}, u32[]{:S(2)}, u32[]{:S(2)}) async-start(bf16[64,2,2560]{2,1,0:T(2,128)(2,1)} %copy.46), calls=%async_computation.1 | async-start | bytes 1310720 | tf_op jit(solution)/shard_map/all_to_all | solution.py:56
  281.1 45.2 %reduce-scatter.4.cloned.1.call-start = ((), (), s32[]{:S(2)}) async-start(), calls=%async_computation.6 | async-start | bytes 819200
  305.3 117.8 %copy-start.10 = (f32[2560]{0:T(1024)S(1)}, f32[2560]{0:T(1024)}, u32[]{:S(2)}) copy-start(f32[2560]{0:T(1024)} %param.26) | copy-start | bytes 30724
  306.5 114.2 %all-gather.5.cloned.1.call-start = ((), (), s32[]{:S(2)}) async-start(), calls=%async_computation.5 | async-start | bytes 2662400 | tf_op jit(solution)/shard_map/all_gather | solution.py:159
  420.6 2.5 copy-start.1
Sparse Core Ops, SparseCore 0:
  134.7 41.5 all-reduce.1
  179.4 80.8 all-gather.2
  306.6 19.6 reduce-scatter.3
  338.4 82.1 all-gather.4
